TPU v7x, 32 devices: a whole 2x2x4 slice. The times are simulated.
32 devices in a mesh: ab: 2 (over y), cd: 16 (over z, x, core).
Axes of the slice: x: 2, y: 2, z: 4, core: 2. Of those that a mesh axis runs over, the one named last changes fastest.
Arguments:
- amplitudes: float32 [768, 16384], P('cd', 'ab'), may hold values from -1.25 to 1.25
- driver: float32 [768, 16384], P('cd', 'ab'), may hold values from -6 to 6
- ladder: bfloat16 [16384, 16384], P('ab', 'cd'), may hold values from -0.125 to 0.125
- block_mask: int32 [128, 128], P('ab', 'cd'), may hold values 0 or 1
- pair_list: int32 [768], replicated, may hold values from 0 to 1023, as said below
- occ_energy: float32 [32], replicated, may hold values from -2 to -0.5
- virt_energy: float32 [128], replicated, may hold values from 0.5 to 3
Outputs:
- new_amplitudes: float32 [768, 16384], P('cd', 'ab')
Inputs may be any that keep to these rules, and one draw needn't show every extreme that they name: `pair_list`: the entries are distinct occupied pairs i * 32 + j. Rows come in aligned blocks of two: a pair with i != j shares its block with the pair (j, i); pairs with i == j stand two to a block. Pairs 0 and 1023 are always listed.
All inputs are finite; a program needn't handle non-finite values. No bound on the sum of `block_mask` on one device may be relied on, other than what follows from the above.
Results may differ from a plain program's by a relative error of at most 0.008.
Values may be sent and summed in bfloat16 or wider, within the bound.
A program may use at most 128 MiB of HBM per device.

v0:
```python
import jax
import jax.numpy as jnp
from jax import lax
from jax.sharding import PartitionSpec as P

NV = 128
NOCC = 32
BLK = 128
ITERS = 2


def flip_tiles(tiles, tile_width):
    row_count, tile_count = tiles.shape[:2]
    turned = jnp.swapaxes(tiles.reshape(row_count, tile_count, tile_width, tile_width), 2, 3)
    return turned.reshape(row_count, tile_count * tile_width * tile_width)


def body(amplitudes, driver, ladder, block_mask, pair_list, occ_energy, virt_energy):
    ab_count = lax.axis_size("ab")
    ab_index = lax.axis_index("ab")
    cd_index = lax.axis_index("cd")
    rows_dev, cols_dev = amplitudes.shape
    out_rows, in_cols = ladder.shape
    tile_width = NV // ab_count
    tile_area = tile_width * tile_width
    weights = ladder.reshape(out_rows // BLK, BLK, in_cols // BLK, BLK)
    weights = (weights * block_mask.astype(jnp.bfloat16)[:, None, :, None]).reshape(
        out_rows, in_cols
    )
    pairs_local = ab_index * cols_dev + jnp.arange(cols_dev, dtype=jnp.int32)
    big_a = pairs_local // (tile_width * NV)
    big_b = pairs_local // tile_area % ab_count
    first = big_a * tile_width + pairs_local // tile_width % tile_width
    second = big_b * tile_width + pairs_local % tile_width
    virt_index = jnp.arange(NV, dtype=jnp.int32)
    picks = (first[:, None] == virt_index).astype(jnp.float32) + (
        second[:, None] == virt_index
    ).astype(jnp.float32)
    col_energy = jnp.dot(picks, virt_energy, precision=lax.Precision.HIGHEST)
    row_pairs = lax.dynamic_slice_in_dim(pair_list, cd_index * rows_dev, rows_dev)
    occ_index = jnp.arange(NOCC, dtype=jnp.int32)
    occ_picks = (row_pairs[:, None] // NOCC == occ_index).astype(jnp.float32)
    occ_picks = occ_picks + (row_pairs[:, None] % NOCC == occ_index).astype(jnp.float32)
    row_energy = jnp.dot(occ_picks, occ_energy, precision=lax.Precision.HIGHEST)
    denominator = col_energy[None, :] - row_energy[:, None]
    local_diagonal = row_pairs // NOCC == row_pairs % NOCC
    row_index = jnp.arange(rows_dev, dtype=jnp.int32)
    mirror_row = jnp.where(local_diagonal, row_index, row_index ^ 1)
    row_swap = (mirror_row[:, None] == row_index).astype(jnp.bfloat16)
    state = amplitudes
    for step in range(ITERS):
        rounded = state.astype(jnp.bfloat16)
        regrouped = lax.all_to_all(rounded, "cd", split_axis=1, concat_axis=0, tiled=True)
        partial_value = lax.dot_general(
            lax.all_gather(regrouped, "ab", axis=1, tiled=True),
            weights,
            (((1,), (1,)), ((), ())),
            preferred_element_type=jnp.float32,
        )
        received = lax.psum_scatter(
            partial_value.astype(jnp.bfloat16), "cd", scatter_dimension=0, tiled=True
        )
        swapped = jnp.dot(row_swap, received, preferred_element_type=jnp.float32)
        tiles = lax.all_to_all(
            swapped.astype(jnp.bfloat16).reshape(rows_dev, ab_count, tile_area),
            "ab",
            split_axis=1,
            concat_axis=1,
            tiled=True,
        )
        symmetric = received.astype(jnp.float32) + flip_tiles(tiles, tile_width).astype(jnp.float32)
        state = (driver + symmetric) / denominator
    return state


def solution(mesh):
    placed = (P("cd", "ab"), P("cd", "ab"), P("ab", "cd"), P("ab", "cd"), P(), P(), P())
    return jax.shard_map(body, mesh=mesh, in_specs=placed, out_specs=P("cd", "ab"), check_vma=False)
```

profile of v0, /device:TPU:0, one launch (start us, length us, event | category | flops | bytes accessed | tf_op | source)
XLA Modules:
  0.0 506.5 jit_solution(11198391696417357768)
XLA Ops:
  6.5 1.5 convert_element_type.68
  8.1 0.1 copy.81
  8.1 27.4 %all_to_all.48 = bf16[48,16,512]{2,0,1:T(8,128)(2,1)} all-to-all(bf16[48,16,512]{2,0,1:T(8,128)(2,1)S(1)} %bitcast.62), channel_id=1, replica_groups=mesh['ab'=2,'cd'=16] {'cd'}, dimensions={1} | all-to-all | bytes 1572864 | tf_op jit(solution)/shard_map/all_to_all | solution.py:53
  35.6 0.1 copy.52
  35.7 26.5 %all-gather.3.cloned.1.call-done = bf16[768,1024]{1,0:T(8,128)(2,1)} async-done(((bf16[768,512]{1,0:T(8,128)(2,1)}), bf16[768,1024]{1,0:T(8,128)(2,1)}) %all-gather.3.cloned.1.call-update) | async-done | bytes 1572880 | tf_op jit(solution)/shard_map/all_gather | solution.py:55
  62.2 6.1 %mul.31 = bf16[64,128,8,128]{3,2,1,0:T(8,128)(2,1)} broadcast(bf16[64,8]{1,0:T(8,128)(2,1)S(1)} %copy.52), dimensions={0,2} | broadcast | bytes 16778240 | tf_op jit(solution)/shard_map/mul | solution.py:27
  68.3 22.4 %fusion = bf16[768,8192]{0,1:T(8,128)(2,1)} fusion(bf16[768,1024]{1,0:T(8,128)(2,1)S(1)} %copy-done.3, bf16[8192,1024]{1,0:T(8,128)(2,1)} %param.9, bf16[1024,8,8,128]{3,2,1,0:T(8,128)(2,1)} %bitcast.55), kind=kOutput, calls=%fused_computation.3 | convolution fusion | flops 12899581952 | bytes 47710208 | tf_op jit(solution)/shard_map/dot_general | solution.py:54
  90.7 16.7 %copy.62 = bf16[768,8192]{1,0:T(8,128)(2,1)} copy(bf16[768,8192]{0,1:T(8,128)(2,1)} %fusion) | data formatting | bytes 25165824
  107.4 0.8 compare_select_fusion
  108.2 134.3 %reduce-scatter.7.cloned.1.call-done = bf16[48,8192]{1,0:T(8,128)(2,1)} async-done(((bf16[768,8192]{1,0:T(8,128)(2,1)}), bf16[48,8192]{1,0:T(8,128)(2,1)}) %reduce-scatter.7.cloned.1.call-update) | async-done | bytes 786448
  242.5 1.5 convolution_convert_fusion.3
  244.0 0.9 copy.80
  244.9 3.5 all-to-all-start.1
  248.5 0.1 fusion.10
  248.6 0.2 convolution_bitcast_fusion
  248.8 6.4 %fusion.1 = f32[1,8192]{1,0:T(1,128)S(1)} fusion(s32[8192]{0:T(1024)S(1)} %get-tuple-element.9, s32[8192]{0:T(1024)S(1)} %get-tuple-element.8, f32[128]{0:T(128)S(1)} %copy-done), kind=kOutput, calls=%fused_computation.6 | convolution fusion | flops 17825792 | bytes 98816 | tf_op jit(solution)/shard_map/dot_general | solution.py:39
  255.3 3.5 all-to-all-done.1
  258.7 2.4 reshape.139
  261.1 2.4 copy.56
  263.5 1.9 reshape.137
  265.4 2.5 fusion.7
  268.0 25.0 %all_to_all.49 = bf16[48,16,512]{2,0,1:T(8,128)(2,1)} all-to-all(bf16[48,16,512]{2,0,1:T(8,128)(2,1)S(1)} %bitcast.63), channel_id=1, replica_groups=mesh['ab'=2,'cd'=16] {'cd'}, dimensions={1} | all-to-all | bytes 1572864 | tf_op jit(solution)/shard_map/all_to_all | solution.py:53
  293.0 0.2 reduce-scatter.9.cloned.1.call-start
  293.2 25.5 %all-gather.5.cloned.1.call-done = bf16[768,1024]{1,0:T(8,128)(2,1)} async-done(((bf16[768,512]{1,0:T(8,128)(2,1)}), bf16[768,1024]{1,0:T(8,128)(2,1)}) %all-gather.5.cloned.1.call-update) | async-done | bytes 1572880 | tf_op jit(solution)/shard_map/all_gather | solution.py:55
  318.7 21.7 %convolution_convert_fusion = bf16[768,8192]{1,0:T(8,128)(2,1)} fusion(bf16[768,1024]{1,0:T(8,128)(2,1)} %all-gather.5.cloned.1.call-done, bf16[8192,1024]{1,0:T(8,128)(2,1)} %param.9, bf16[1024,8,8,128]{3,2,1,0:T(8,128)(2,1)} %bitcast.56), kind=kOutput, calls=%fused_computation.1 | convolution fusion | flops 12899581952 | bytes 47710208 | tf_op jit(solution)/shard_map/dot_general | solution.py:54
  340.4 135.0 %reduce-scatter.9.cloned.1.call-done = bf16[48,8192]{1,0:T(8,128)(2,1)} async-done(((bf16[768,8192]{1,0:T(8,128)(2,1)}), bf16[48,8192]{1,0:T(8,128)(2,1)}) %reduce-scatter.9.cloned.1.call-update) | async-done | bytes 786448
  475.4 1.5 convolution_convert_fusion.2
  477.0 12.7 %all_to_all.50 = bf16[48,2,4096]{2,0,1:T(8,128)(2,1)S(1)} all-to-all(bf16[48,2,4096]{2,0,1:T(8,128)(2,1)S(1)} %bitcast.65), channel_id=1, replica_groups=mesh['ab'=2,'cd'=16] {'ab'}, dimensions={1} | all-to-all | bytes 1572864 | tf_op jit(solution)/shard_map/all_to_all | solution.py:64
  489.7 2.4 reshape.140
  492.1 2.4 copy.61
  494.5 1.9 reshape.138
  496.4 3.6 subtract_divide_fusion
  (20 shorter events, 0.3 us)
Async XLA Ops:
  6.5 242.3 %copy-start = (f32[128]{0:T(128)S(1)}, f32[128]{0:T(128)}, u32[]{:S(2)}) copy-start(f32[128]{0:T(128)} %param.13) | copy-start | bytes 1540
  6.5 29.1 %copy-start.2 = (s32[64,8]{0,1:T(8,128)S(1)}, s32[64,8]{0,1:T(8,128)}, u32[]{:S(2)}) copy-start(s32[64,8]{0,1:T(8,128)} %param.10) | copy-start | bytes 6148
  6.5 55.7 %all-gather.3.cloned.1.call-start = ((), (), s32[]{:S(2)}) async-start(), calls=%async_computation.6 | async-start | bytes 2359296 | tf_op jit(solution)/shard_map/all_gather | solution.py:55
  35.6 206.9 %reduce-scatter.7.cloned.1.call-start = ((), (), s32[]{:S(2)}) async-start(), calls=%async_computation.8 | async-start | bytes 13369344
  62.2 6.1 %copy-start.3 = (bf16[768,1024]{1,0:T(8,128)(2,1)S(1)}, bf16[768,1024]{1,0:T(8,128)(2,1)}, u32[]{:S(2)}) copy-start(bf16[768,1024]{1,0:T(8,128)(2,1)} %all-gather.3.cloned.1.call-done) | copy-start | bytes 4718596
  107.4 141.2 %copy-start.4 = (f32[32]{0:T(128)S(1)}, f32[32]{0:T(128)}, u32[]{:S(2)}) copy-start(f32[32]{0:T(128)} %param.12) | copy-start | bytes 388
  244.9 13.8 %all-to-all-start.1 = ((bf16[48,2,4096]{2,0,1:T(8,128)(2,1)}), bf16[48,2,4096]{2,0,1:T(8,128)(2,1)S(1)}, u32[]{:S(2)}, u32[]{:S(2)}) async-start(bf16[48,2,4096]{2,0,1:T(8,128)(2,1)} %bitcast.53), calls=%async_computation.1 | async-start | bytes 1572864 | tf_op jit(solution)/shard_map/all_to_all | solution.py:64
  248.5 70.2 %all-gather.5.cloned.1.call-start = ((), (), s32[]{:S(2)}) async-start(), calls=%async_computation.7 | async-start | bytes 2359296 | tf_op jit(solution)/shard_map/all_gather | solution.py:55
  293.0 182.4 %reduce-scatter.9.cloned.1.call-start = ((), (), s32[]{:S(2)}) async-start(), calls=%async_computation.9 | async-start | bytes 13369344
  494.5 5.5 %copy-start.1 = (f32[128]{0:T(128)S(1)}, f32[128]{0:T(128)}, u32[]{:S(2)}) copy-start(f32[128]{0:T(128)} %param.13) | copy-start | bytes 1540
Sparse Core Ops, SparseCore 0:
  35.7 26.4 all-gather.2
  107.5 134.9 reduce-scatter.6
  293.1 25.5 all-gather.4
  340.5 134.8 reduce-scatter.8
where the time goes:
time: 507 us
  waiting for transfers between devices  325 us (64%)
  blocking collectives  65.1 us (13%)
  matrix products  53.8 us (11%)
  local copies, waits for them, and re-layouts  37.3 us (7%)
  between operations  13.3 us (3%)
  other arithmetic  8.42 us (2%)
    unnamed x6, waiting for transfers between devices  269 us
    all_to_all x2, blocking collectives, body(): lax.all_to_all(rounded, 'cd', split_axis=1, concat_axis=0, tiled=True)  52.4 us
    all_gather x2, waiting for transfers between devices, body(): lax.all_gather(regrouped, 'ab', axis=1, tiled=True)  52 us
    dot_general x2, matrix products, body(): lax.dot_general(lax.all_gather(regrouped, 'ab', axis=1, tiled=True), weig...  44.1 us
    unnamed x11, local copies, waits for them, and re-layouts  16.7 us
    convert_element_type x6, local copies, waits for them, and re-layouts, body(): flip_tiles(tiles, tile_width).astype(jnp.float32)  13.3 us
    all_to_all x1, blocking collectives, body(): lax.all_to_all(swapped.astype(jnp.bfloat16).reshape(rows_dev, ab_count, t...  12.7 us
  transfers between devices with their start and end apart: 5, of which 5 were waited for; matrix products, arithmetic and copies ran while one was open for 1% of the time, Pallas kernels for 0%

commit v1 on v0

--- a/solution.py
+++ b/solution.py
@@ -7,6 +7,28 @@
 NOCC = 32
 BLK = 128
 ITERS = 2
+
+
+def joined_along(parts, dim):
+    parts = jnp.moveaxis(parts, 0, dim)
+    shape = parts.shape
+    return parts.reshape(*shape[:dim], shape[dim] * shape[dim + 1], *shape[dim + 2 :])
+
+
+def doubled(x, axis):
+    size = lax.axis_size(axis)
+    blocks = x[None]
+    for level in range(size.bit_length() - 1):
+        stride = 1 << level
+        other = lax.ppermute(blocks, axis, [(i, i ^ stride) for i in range(size)])
+        both = jnp.stack([blocks, other])
+        upper = lax.axis_index(axis) >> level & 1
+        blocks = jnp.where(upper == 0, both, both[::-1]).reshape(-1, *x.shape)
+    return blocks
+
+
+def gather_by_bits(array, axis, dim):
+    return joined_along(doubled(array, axis), dim)
 
 
 def flip_tiles(tiles, tile_width):
@@ -52,7 +74,7 @@
         rounded = state.astype(jnp.bfloat16)
         regrouped = lax.all_to_all(rounded, "cd", split_axis=1, concat_axis=0, tiled=True)
         partial_value = lax.dot_general(
-            lax.all_gather(regrouped, "ab", axis=1, tiled=True),
+            gather_by_bits(regrouped, "ab", 1),
             weights,
             (((1,), (1,)), ((), ())),
             preferred_element_type=jnp.float32,

time: 507 us -> 476 us (0.939)
  waiting for transfers between devices: 325 us -> 308 us
  local copies, waits for them, and re-layouts: 37.3 us -> 22.2 us
    unnamed x6 -> x2, waiting for transfers between devices: 269 us -> 0.03 us
    reduce_scatter x0 -> x2, waiting for transfers between devices: none -> 266 us  [body(): lax.psum_scatter(partial_value.astype(jnp.bfloat16), 'cd', scatter_dimens...]
    all_gather x2 -> x0, waiting for transfers between devices: 52 us -> none  [body(): lax.all_gather(regrouped, 'ab', axis=1, tiled=True)]
    ppermute x0 -> x2, waiting for transfers between devices: none -> 38.8 us  [doubled(): other = lax.ppermute(blocks, axis, [(i, i ^ stride) for i in range(size)])]
    unnamed x11 -> x8, local copies, waits for them, and re-layouts: 16.7 us -> 0.02 us
  transfers between devices with their start and end apart: 5 -> 5, of which waited for: 5 -> 5; matrix products, arithmetic and copies ran while one was open for 1% -> 2% of each run, Pallas kernels for 0% -> 0%
where the time goes in v1:
time: 476 us
  waiting for transfers between devices  308 us (65%)
  blocking collectives  64.9 us (14%)
  matrix products  52.5 us (11%)
  local copies, waits for them, and re-layouts  22.2 us (5%)
  between operations  13.6 us (3%)
  other arithmetic  9.27 us (2%)
  starting transfers between devices  5.39 us (1%)
    reduce_scatter x2, waiting for transfers between devices, body(): lax.psum_scatter(partial_value.astype(jnp.bfloat16), 'cd', scatter_dimens...  266 us
    all_to_all x2, blocking collectives, body(): lax.all_to_all(rounded, 'cd', split_axis=1, concat_axis=0, tiled=True)  52.2 us
    dot_general x2, matrix products, body(): lax.dot_general(gather_by_bits(regrouped, 'ab', 1), weights, (((1,), (1,)...  42.8 us
    ppermute x2, waiting for transfers between devices, doubled(): other = lax.ppermute(blocks, axis, [(i, i ^ stride) for i in range(size)])  38.8 us
    convert_element_type x6, local copies, waits for them, and re-layouts, body(): flip_tiles(tiles, tile_width).astype(jnp.float32)  13.4 us
    all_to_all x1, blocking collectives, body(): lax.all_to_all(swapped.astype(jnp.bfloat16).reshape(rows_dev, ab_count, t...  12.7 us
  transfers between devices with their start and end apart: 5, of which 5 were waited for; matrix products, arithmetic and copies ran while one was open for 2% of the time, Pallas kernels for 0%

profile of v1, /device:TPU:0, one launch (start us, length us, event | category | flops | bytes accessed | tf_op | source)
XLA Modules:
  0.0 476.0 jit_solution(6555994767356325950)
XLA Ops:
  6.5 1.5 convert_element_type.64
  8.1 27.3 %all_to_all.42 = bf16[48,16,512]{2,0,1:T(8,128)(2,1)S(1)} all-to-all(bf16[48,16,512]{2,0,1:T(8,128)(2,1)S(1)} %bitcast.72), channel_id=1, replica_groups=mesh['ab'=2,'cd'=16] {'cd'}, dimensions={1} | all-to-all | bytes 1572864 | tf_op jit(solution)/shard_map/all_to_all | solution.py:75
  35.4 1.5 collective-permute-start
  37.1 18.7 %collective-permute-done = bf16[1,768,512]{2,1,0:T(8,128)(2,1)S(1)} collective-permute-done((bf16[1,768,512]{2,1,0:T(8,128)(2,1)S(1)}, bf16[1,768,512]{2,1,0:T(8,128)(2,1)S(1)}, u32[]{:S(2)}, u32[]{:S(2)}) %collective-permute-start) | collective-permute-done | bytes 786464 | tf_op jit(solution)/shard_map/ppermute | solution.py:23
  56.0 0.3 fusion.7
  56.2 0.7 copy.28
  57.0 6.1 %mul.31 = bf16[64,128,8,128]{3,2,1,0:T(8,128)(2,1)} broadcast(bf16[64,8]{1,0:T(8,128)(2,1)S(1)} %copy.29), dimensions={0,2} | broadcast | bytes 16778240 | tf_op jit(solution)/shard_map/mul | solution.py:49
  63.1 21.4 %convolution_convert_fusion.1 = bf16[768,8192]{1,0:T(8,128)(2,1)} fusion(bf16[768,1024]{0,1:T(8,128)(2,1)S(1)} %bitcast.82, bf16[8192,1024]{1,0:T(8,128)(2,1)} %param.9, bf16[1024,8,8,128]{3,2,1,0:T(8,128)(2,1)} %bitcast.67), kind=kOutput, calls=%fused_computation.2 | convolution fusion | flops 12899581952 | bytes 47710208 | tf_op jit(solution)/shard_map/dot_general | solution.py:76
  84.5 0.8 compare_select_fusion
  85.3 133.0 %reduce-scatter.3.cloned.1.call-done = bf16[48,8192]{1,0:T(8,128)(2,1)} async-done(((bf16[768,8192]{1,0:T(8,128)(2,1)}), bf16[48,8192]{1,0:T(8,128)(2,1)}) %reduce-scatter.3.cloned.1.call-update) | async-done | bytes 786448 | tf_op jit(solution)/shard_map/reduce_scatter | solution.py:82
  218.3 1.5 convolution_convert_fusion.3
  219.8 0.9 copy.50
  220.8 3.5 all-to-all-start.1
  224.7 6.4 %fusion = f32[1,8192]{1,0:T(1,128)S(1)} fusion(s32[8192]{0:T(1024)S(1)} %get-tuple-element.9, s32[8192]{0:T(1024)S(1)} %get-tuple-element.8, f32[128]{0:T(128)S(1)} %copy-done), kind=kOutput, calls=%fused_computation.5 | convolution fusion | flops 17825792 | bytes 98816 | tf_op jit(solution)/shard_map/dot_general | solution.py:61
  231.1 3.5 all-to-all-done.1
  234.6 2.4 reshape.159
  237.0 2.4 copy.31
  239.4 1.9 reshape.157
  241.3 2.5 fusion.6
  243.8 24.9 %all_to_all.43 = bf16[48,16,512]{2,0,1:T(8,128)(2,1)S(1)} all-to-all(bf16[48,16,512]{2,0,1:T(8,128)(2,1)S(1)} %bitcast.73), channel_id=1, replica_groups=mesh['ab'=2,'cd'=16] {'cd'}, dimensions={1} | all-to-all | bytes 1572864 | tf_op jit(solution)/shard_map/all_to_all | solution.py:75
  268.7 0.3 collective-permute-start.1
  269.0 20.1 %collective-permute-done.1 = bf16[1,768,512]{2,1,0:T(8,128)(2,1)S(1)} collective-permute-done((bf16[1,768,512]{2,1,0:T(8,128)(2,1)S(1)}, bf16[1,768,512]{2,1,0:T(8,128)(2,1)S(1)}, u32[]{:S(2)}, u32[]{:S(2)}) %collective-permute-start.1) | collective-permute-done | bytes 786464 | tf_op jit(solution)/shard_map/ppermute | solution.py:23
  289.2 0.3 fusion.8
  289.5 0.7 copy.33
  290.2 21.4 %convolution_convert_fusion = bf16[768,8192]{1,0:T(8,128)(2,1)} fusion(bf16[768,1024]{0,1:T(8,128)(2,1)S(1)} %bitcast.83, bf16[8192,1024]{1,0:T(8,128)(2,1)} %param.9, bf16[1024,8,8,128]{3,2,1,0:T(8,128)(2,1)} %bitcast.68), kind=kOutput, calls=%fused_computation.1 | convolution fusion | flops 12899581952 | bytes 47710208 | tf_op jit(solution)/shard_map/dot_general | solution.py:76
  311.6 132.9 %reduce-scatter.5.cloned.1.call-done = bf16[48,8192]{1,0:T(8,128)(2,1)} async-done(((bf16[768,8192]{1,0:T(8,128)(2,1)}), bf16[48,8192]{1,0:T(8,128)(2,1)}) %reduce-scatter.5.cloned.1.call-update) | async-done | bytes 786448 | tf_op jit(solution)/shard_map/reduce_scatter | solution.py:82
  444.5 1.5 convolution_convert_fusion.2
  446.1 12.7 %all_to_all.44 = bf16[48,2,4096]{2,0,1:T(8,128)(2,1)S(1)} all-to-all(bf16[48,2,4096]{2,0,1:T(8,128)(2,1)S(1)} %bitcast.75), channel_id=1, replica_groups=mesh['ab'=2,'cd'=16] {'ab'}, dimensions={1} | all-to-all | bytes 1572864 | tf_op jit(solution)/shard_map/all_to_all | solution.py:86
  458.8 2.4 reshape.160
  461.2 2.4 copy.35
  463.6 1.9 reshape.158
  465.5 3.6 subtract_divide_fusion
  (21 shorter events, 1.0 us)
Async XLA Ops:
  6.5 218.1 %copy-start = (f32[128]{0:T(128)S(1)}, f32[128]{0:T(128)}, u32[]{:S(2)}) copy-start(f32[128]{0:T(128)} %param.13) | copy-start | bytes 1540
  6.5 211.7 %reduce-scatter.3.cloned.1.call-start = ((), (), s32[]{:S(2)}) async-start(), calls=%async_computation.6 | async-start | bytes 13369344 | tf_op jit(solution)/shard_map/reduce_scatter | solution.py:82
  8.0 28.9 %copy-start.2 = (s32[64,8]{0,1:T(8,128)S(1)}, s32[64,8]{0,1:T(8,128)}, u32[]{:S(2)}) copy-start(s32[64,8]{0,1:T(8,128)} %param.10) | copy-start | bytes 6148
  35.4 20.4 %collective-permute-start = (bf16[1,768,512]{2,1,0:T(8,128)(2,1)S(1)}, bf16[1,768,512]{2,1,0:T(8,128)(2,1)S(1)}, u32[]{:S(2)}, u32[]{:S(2)}) collective-permute-start(bf16[1,768,512]{2,1,0:T(8,128)(2,1)S(1)} %bitcast.77), channel_id=1, source_target_pairs={{0,16},{16,0},{1,17},{17,1},{2,18},{18,2},{3,19},{19,3},{4,20},{20... | collective-permute-start | bytes 2359304 | tf_op jit(solution)/shard_map/ppermute | solution.py:23
  219.8 4.6 copy-start.3
  220.8 13.8 %all-to-all-start.1 = ((bf16[48,2,4096]{2,0,1:T(8,128)(2,1)}), bf16[48,2,4096]{2,0,1:T(8,128)(2,1)S(1)}, u32[]{:S(2)}, u32[]{:S(2)}) async-start(bf16[48,2,4096]{2,0,1:T(8,128)(2,1)} %bitcast.65), calls=%async_computation.2 | async-start | bytes 1572864 | tf_op jit(solution)/shard_map/all_to_all | solution.py:86
  224.3 220.2 %reduce-scatter.5.cloned.1.call-start = ((), (), s32[]{:S(2)}) async-start(), calls=%async_computation.7 | async-start | bytes 13369344 | tf_op jit(solution)/shard_map/reduce_scatter | solution.py:82
  268.7 20.4 %collective-permute-start.1 = (bf16[1,768,512]{2,1,0:T(8,128)(2,1)S(1)}, bf16[1,768,512]{2,1,0:T(8,128)(2,1)S(1)}, u32[]{:S(2)}, u32[]{:S(2)}) collective-permute-start(bf16[1,768,512]{2,1,0:T(8,128)(2,1)S(1)} %bitcast.79), channel_id=1, source_target_pairs={{0,16},{16,0},{1,17},{17,1},{2,18},{18,2},{3,19},{19,3},{4,20},{20... | collective-permute-start | bytes 2359304 | tf_op jit(solution)/shard_map/ppermute | solution.py:23
  463.6 5.5 %copy-start.1 = (f32[128]{0:T(128)S(1)}, f32[128]{0:T(128)}, u32[]{:S(2)}) copy-start(f32[128]{0:T(128)} %param.13) | copy-start | bytes 1540
Sparse Core Ops, SparseCore 0:
  84.6 133.6 reduce-scatter.2
  311.8 132.6 reduce-scatter.4
